TPU v7x, 32 devices: a whole 2x2x4 slice. The times are simulated.
32 devices in a mesh: group: 4 (over z), dev: 8 (over y, x, core).
Axes of the slice: x: 2, y: 2, z: 4, core: 2. Of those that a mesh axis runs over, the one named last changes fastest.
Arguments:
- positions: float32 [3, 1024, 256], P(None, ('group', 'dev')), may hold values from -3 to 3
- velocities: float32 [3, 1024, 256], P(None, ('group', 'dev')), may hold values from -3 to 3
- masses: float32 [1024, 256], P(('group', 'dev')), may hold values from 0.005 to 0.05
- counts: int32 [1024], P(('group', 'dev')), may hold values from 64 to 256, as said below
- walls: int32 [1024, 256], P(('group', 'dev')), may hold values 0 or 1
- neighbours: int32 [1024, 3], P(('group', 'dev')), may hold values from 0 to 55, as said below
- send_cells: int32 [4, 8, 8, 2], P('group', 'dev'), may hold values from -1 to 31, as said below
- owners: int32 [4, 256], P('group'), may hold values from 0 to 7, as said below
Outputs:
- new_state: float32 [6, 1024, 256], P(None, ('group', 'dev'))
- new_density: float32 [1024, 256], P(('group', 'dev'))
Inputs may be any that keep to these rules, and one draw needn't show every extreme that they name: `counts`: every device holds at least one cell with 256 particles. `send_cells`: A device never sends to itself; slot 0 to every other device of its group holds a cell. `neighbours`: A cell never names its own row; on each device every rim row and every filled incoming slot is named at least once, and no empty incoming slot is named. `owners`: each device of a group owns exactly 32 cells afterwards; each device keeps 32 - 2 * 2 of its cells and hands exactly 2 cells to each of 2 other devices of its group, and none to the rest.
All inputs are finite; a program needn't handle non-finite values. No bound on the sum of `walls` on one device may be relied on, other than what follows from the above.
Results may differ from a plain program's by a relative error of at most 0.0003.
Values sent between devices are 32-bit elements; how exact they have to be, the bound alone decides.
A program may use at most 64 MiB of HBM per device.

v0:
```python
import jax
import jax.numpy as jnp
from jax import lax
from jax.sharding import PartitionSpec as P

RIM_CELLS = 4
SUPPORT = 4.0
STIFFNESS = 2.0
REST_DENSITY = 0.8
VISCOSITY = 0.5
COHESION = 0.3
ADHESION = 0.8
GRAVITY = 1.0
TIME_STEP = 0.5


def with_halo(cells, sides, width):
    for axis, dim in sides:
        count = lax.axis_size(axis)
        ends = count - 1
        head = lax.slice_in_dim(cells, 0, width, axis=dim)
        tail = lax.slice_in_dim(cells, cells.shape[dim] - width, cells.shape[dim], axis=dim)
        cells = jnp.concatenate(
            [
                lax.ppermute(tail, axis, [(i, (i + 1) % count) for i in range(ends)]),
                cells,
                lax.ppermute(head, axis, [((i + 1) % count, i) for i in range(ends)]),
            ],
            axis=dim,
        )
    return cells


def pair_density(own_pos, lookup, columns):
    remote = lookup[:, columns, :]
    distance = jnp.zeros(
        (own_pos.shape[1], own_pos.shape[2], columns.shape[1], lookup.shape[2]), jnp.float32
    )
    for component in range(3):
        offset = own_pos[component][:, :, None, None] - remote[component][:, None, :, :]
        distance = distance + offset * offset
    weight = jnp.maximum(1.0 - distance / SUPPORT, 0.0)
    return jnp.sum(remote[3][:, None, :, :] * weight * weight * weight, axis=(2, 3))


def pair_force(own_pos, own_vel, own_q, lookup, columns):
    remote = lookup[:, columns, :]
    distance = jnp.zeros(
        (own_pos.shape[1], own_pos.shape[2], columns.shape[1], lookup.shape[2]), jnp.float32
    )
    offsets = []
    for component in range(3):
        offset = own_pos[component][:, :, None, None] - remote[component][:, None, :, :]
        offsets.append(offset)
        distance = distance + offset * offset
    weight = jnp.maximum(1.0 - distance / SUPPORT, 0.0)
    cube = weight * weight * weight
    pushes = (
        remote[6][:, None]
        * (own_q[:, :, None, None] + remote[8][:, None])
        * (6.0 / SUPPORT)
        * weight
        * weight
        - remote[7][:, None] * weight
    )
    damping = VISCOSITY * remote[6][:, None] * cube
    total_damping = jnp.sum(damping, axis=(2, 3))
    rows = []
    for component in range(3):
        rows.append(
            jnp.sum(
                offsets[component] * pushes + damping * remote[3 + component][:, None], axis=(2, 3)
            )
            - own_vel[component] * total_damping
        )
    return jnp.stack(rows, 0)


def shards(positions, velocities, masses, counts, walls, neighbours, send_cells, owners):
    cell_count = positions.shape[1]
    block_width = positions.shape[2]
    peer_count = lax.axis_size("dev")
    particle_slot = lax.broadcasted_iota(jnp.int32, (cell_count, block_width), 1)
    active = (particle_slot < counts[:, None]).astype(jnp.float32)
    wall_mask = walls.astype(jnp.float32) * active
    fluid_mask = active - wall_mask
    mass_eff = masses * active
    bond = mass_eff * (COHESION + (ADHESION - COHESION) * wall_mask)
    send_list = send_cells[0, 0].reshape(-1)
    present = (send_list >= 0).astype(jnp.float32)
    chosen = jnp.maximum(send_list, 0)

    def outgoing(field):
        return field[:, chosen, :] * present[None, :, None]

    def joined(padded, arrived):
        return jnp.concatenate([padded, arrived], 1)

    dens_field = jnp.concatenate([positions, mass_eff[None]], 0)
    dens_table = joined(
        with_halo(dens_field, (("group", 1),), RIM_CELLS),
        lax.all_to_all(outgoing(dens_field), "dev", split_axis=1, concat_axis=1, tiled=True),
    )
    cell_blocks = jnp.arange(cell_count, dtype=jnp.int32).reshape(-1, 4)

    def density_block(cell_ids):
        columns = jnp.concatenate([RIM_CELLS + cell_ids[:, None], neighbours[cell_ids]], 1)
        return pair_density(positions[:, cell_ids, :], dens_table, columns)

    density = lax.map(density_block, cell_blocks).reshape(cell_count, block_width)
    safe_rho = active * density + (1.0 - active)
    pressure_q = active * STIFFNESS * (density - REST_DENSITY) / (safe_rho * safe_rho)
    force_field = jnp.concatenate(
        [positions, velocities, mass_eff[None], bond[None], pressure_q[None]], 0
    )
    force_table = joined(
        with_halo(force_field, (("group", 1),), RIM_CELLS),
        lax.all_to_all(outgoing(force_field), "dev", split_axis=1, concat_axis=1, tiled=True),
    )

    def force_block(cell_ids):
        columns = jnp.concatenate([RIM_CELLS + cell_ids[:, None], neighbours[cell_ids]], 1)
        return pair_force(
            positions[:, cell_ids, :],
            velocities[:, cell_ids, :],
            pressure_q[cell_ids],
            force_table,
            columns,
        )

    acceleration = lax.map(force_block, cell_blocks)
    acceleration = jnp.transpose(acceleration, (1, 0, 2, 3)).reshape(3, cell_count, block_width)
    gravity_vec = jnp.array([0.0, 0.0, GRAVITY], jnp.float32)[:, None, None]
    acceleration = acceleration - gravity_vec
    new_vel = velocities + TIME_STEP * fluid_mask[None] * acceleration
    new_pos = positions + TIME_STEP * fluid_mask[None] * new_vel
    moved = jnp.concatenate([new_pos, new_vel, density[None]], 0) * active[None]
    capacity = max(2, cell_count // (2 * peer_count))
    own_index = lax.axis_index("dev")
    group_owner = owners[0]
    own_owners = lax.dynamic_slice_in_dim(group_owner, own_index * cell_count, cell_count)
    one_hot = (own_owners[:, None] == jnp.arange(peer_count, dtype=jnp.int32)[None, :]).astype(
        jnp.int32
    )
    send_rank = jnp.sum((jnp.cumsum(one_hot, 0) - one_hot) * one_hot, 1)
    staying = own_owners == own_index
    slot_index = jnp.where(staying, peer_count * capacity, own_owners * capacity + send_rank)
    outbox = (
        jnp.zeros((7, peer_count * capacity, block_width), jnp.float32)
        .at[:, slot_index, :]
        .set(moved, mode="drop")
    )
    inbox = lax.all_to_all(outbox, "dev", split_axis=1, concat_axis=1, tiled=True)
    arrivals = jnp.sum(
        (group_owner.reshape(peer_count, cell_count) == own_index).astype(jnp.int32), 1
    )
    arrival_start = jnp.cumsum(arrivals) - arrivals
    rank_in = lax.broadcasted_iota(jnp.int32, (peer_count, capacity), 1)
    source_row = lax.broadcasted_iota(jnp.int32, (peer_count, capacity), 0)
    usable = (rank_in < arrivals[:, None]) & (source_row != own_index)
    arrival_slot = jnp.where(usable, arrival_start[:, None] + rank_in, cell_count).reshape(-1)
    keep_slot = jnp.where(staying, arrival_start[own_index] + send_rank, cell_count)
    settled = (
        jnp.zeros((7, cell_count, block_width), jnp.float32)
        .at[:, arrival_slot, :]
        .set(inbox, mode="drop")
    )
    settled = settled.at[:, keep_slot, :].set(moved, mode="drop")
    return (settled[0:6], settled[6])


def solution(mesh):
    return jax.shard_map(
        shards,
        mesh=mesh,
        in_specs=(
            P(None, ("group", "dev"), None),
            P(None, ("group", "dev"), None),
            P(("group", "dev"), None),
            P(("group", "dev")),
            P(("group", "dev"), None),
            P(("group", "dev"), None),
            P("group", "dev", None, None),
            P("group", None),
        ),
        out_specs=(P(None, ("group", "dev"), None), P(("group", "dev"), None)),
        check_vma=False,
    )
```

profile of v0, /device:TPU:0, one launch (start us, length us, event | category | flops | bytes accessed | tf_op | source)
XLA Modules:
  0.0 174.2 jit_solution(14094200770331152187)
XLA Ops:
  3.0 1.0 copy.48
  5.7 5.2 %all-to-all-start = ((f32[4,16,256]{2,0,1:T(4,128)}), f32[4,16,256]{2,0,1:T(4,128)S(1)}, u32[]{:S(2)}, u32[]{:S(2)}) async-start(f32[4,16,256]{2,0,1:T(4,128)} %multiply_bitcast_fusion.1), calls=%async_computation | async-start | bytes 131072 | tf_op jit(solution)/shard_map/all_to_all | solution.py:102
  10.9 3.5 %collective-permute-start = (f32[4,4,256]{2,0,1:T(4,128)S(1)}, f32[4,4,256]{2,0,1:T(4,128)S(1)}, u32[]{:S(2)}, u32[]{:S(2)}) collective-permute-start(f32[4,4,256]{2,0,1:T(4,128)S(1)} %get-tuple-element.204), channel_id=1, source_target_pairs={{0,8},{8,16},{16,24},{1,9},{9,17},{17,25},{2,10},{10,18},{18,26},{... | collective-permute-start | bytes 49160 | tf_op jit(solution)/shard_map/ppermute | solution.py:25
  14.4 1.3 collective-permute-start.1
  18.3 1.7 collective-permute-done.1
  20.1 37.5 %while.20 = (s32[]{:T(128)}, f32[8,4,256]{2,1,0:T(4,128)S(1)}, s32[8,4]{1,0:T(8,128)S(1)}, s32[32,3]{1,0:T(8,128)S(1)}, f32[4,56,256]{2,0,1:T(4,128)S(1)}, /*index=5*/f32[3,32,256]{2,0,1:T(4,128)S(1)}, s32[]{:T(128)}) while((s32[]{:T(128)}, f32[8,4,256]{2,1,0:T(4,128)S(1)}, s32[8,4]{1,0:T(8,128)S(1)}, s32[32,3]{1,0:T(8,128)S(1)}, ...), condition=%wide.region_6.7_spmd, body=%wide.region_4.0_spmd.sunk | while | flops 15729746 | bytes 565941 | solution.py:110
  22.3 2.5 %fusion.57 = f32[4,256]{1,0:T(4,128)S(1)} fusion(f32[4,4,256]{2,1,0:T(4,128)S(1)} %get-tuple-element.339, f32[4,256]{1,0:T(4,128)S(1)} %get-tuple-element.342, f32[4,4,256]{2,1,0:T(4,128)S(1)} %get-tuple-element.343, f32[4,256]{1,0:T(4,128)S(1)} %get-tuple-element.344, f32[4,4,256]{2,1,0:T(4,128)S(1)} %get-tuple-element.347, ...), kind=kLoop, calls=%fused_computation.14.clone.1 | loop fusion | flops 15727616 | bytes 81920 | tf_op jit(solution)/shard_map/while/body/eval_jaxpr/reduce_sum | solution.py:43
  27.0 2.5 %fusion.57 = f32[4,256]{1,0:T(4,128)S(1)} fusion(f32[4,4,256]{2,1,0:T(4,128)S(1)} %get-tuple-element.339, f32[4,256]{1,0:T(4,128)S(1)} %get-tuple-element.342, f32[4,4,256]{2,1,0:T(4,128)S(1)} %get-tuple-element.343, f32[4,256]{1,0:T(4,128)S(1)} %get-tuple-element.344, f32[4,4,256]{2,1,0:T(4,128)S(1)} %get-tuple-element.347, ...), kind=kLoop, calls=%fused_computation.14.clone.1 | loop fusion | flops 15727616 | bytes 81920 | tf_op jit(solution)/shard_map/while/body/eval_jaxpr/reduce_sum | solution.py:43
  31.7 2.5 %fusion.57 = f32[4,256]{1,0:T(4,128)S(1)} fusion(f32[4,4,256]{2,1,0:T(4,128)S(1)} %get-tuple-element.339, f32[4,256]{1,0:T(4,128)S(1)} %get-tuple-element.342, f32[4,4,256]{2,1,0:T(4,128)S(1)} %get-tuple-element.343, f32[4,256]{1,0:T(4,128)S(1)} %get-tuple-element.344, f32[4,4,256]{2,1,0:T(4,128)S(1)} %get-tuple-element.347, ...), kind=kLoop, calls=%fused_computation.14.clone.1 | loop fusion | flops 15727616 | bytes 81920 | tf_op jit(solution)/shard_map/while/body/eval_jaxpr/reduce_sum | solution.py:43
  36.3 2.5 %fusion.57 = f32[4,256]{1,0:T(4,128)S(1)} fusion(f32[4,4,256]{2,1,0:T(4,128)S(1)} %get-tuple-element.339, f32[4,256]{1,0:T(4,128)S(1)} %get-tuple-element.342, f32[4,4,256]{2,1,0:T(4,128)S(1)} %get-tuple-element.343, f32[4,256]{1,0:T(4,128)S(1)} %get-tuple-element.344, f32[4,4,256]{2,1,0:T(4,128)S(1)} %get-tuple-element.347, ...), kind=kLoop, calls=%fused_computation.14.clone.1 | loop fusion | flops 15727616 | bytes 81920 | tf_op jit(solution)/shard_map/while/body/eval_jaxpr/reduce_sum | solution.py:43
  41.0 2.5 %fusion.57 = f32[4,256]{1,0:T(4,128)S(1)} fusion(f32[4,4,256]{2,1,0:T(4,128)S(1)} %get-tuple-element.339, f32[4,256]{1,0:T(4,128)S(1)} %get-tuple-element.342, f32[4,4,256]{2,1,0:T(4,128)S(1)} %get-tuple-element.343, f32[4,256]{1,0:T(4,128)S(1)} %get-tuple-element.344, f32[4,4,256]{2,1,0:T(4,128)S(1)} %get-tuple-element.347, ...), kind=kLoop, calls=%fused_computation.14.clone.1 | loop fusion | flops 15727616 | bytes 81920 | tf_op jit(solution)/shard_map/while/body/eval_jaxpr/reduce_sum | solution.py:43
  45.7 2.5 %fusion.57 = f32[4,256]{1,0:T(4,128)S(1)} fusion(f32[4,4,256]{2,1,0:T(4,128)S(1)} %get-tuple-element.339, f32[4,256]{1,0:T(4,128)S(1)} %get-tuple-element.342, f32[4,4,256]{2,1,0:T(4,128)S(1)} %get-tuple-element.343, f32[4,256]{1,0:T(4,128)S(1)} %get-tuple-element.344, f32[4,4,256]{2,1,0:T(4,128)S(1)} %get-tuple-element.347, ...), kind=kLoop, calls=%fused_computation.14.clone.1 | loop fusion | flops 15727616 | bytes 81920 | tf_op jit(solution)/shard_map/while/body/eval_jaxpr/reduce_sum | solution.py:43
  50.4 2.5 %fusion.57 = f32[4,256]{1,0:T(4,128)S(1)} fusion(f32[4,4,256]{2,1,0:T(4,128)S(1)} %get-tuple-element.339, f32[4,256]{1,0:T(4,128)S(1)} %get-tuple-element.342, f32[4,4,256]{2,1,0:T(4,128)S(1)} %get-tuple-element.343, f32[4,256]{1,0:T(4,128)S(1)} %get-tuple-element.344, f32[4,4,256]{2,1,0:T(4,128)S(1)} %get-tuple-element.347, ...), kind=kLoop, calls=%fused_computation.14.clone.1 | loop fusion | flops 15727616 | bytes 81920 | tf_op jit(solution)/shard_map/while/body/eval_jaxpr/reduce_sum | solution.py:43
  55.1 2.5 %fusion.57 = f32[4,256]{1,0:T(4,128)S(1)} fusion(f32[4,4,256]{2,1,0:T(4,128)S(1)} %get-tuple-element.339, f32[4,256]{1,0:T(4,128)S(1)} %get-tuple-element.342, f32[4,4,256]{2,1,0:T(4,128)S(1)} %get-tuple-element.343, f32[4,256]{1,0:T(4,128)S(1)} %get-tuple-element.344, f32[4,4,256]{2,1,0:T(4,128)S(1)} %get-tuple-element.347, ...), kind=kLoop, calls=%fused_computation.14.clone.1 | loop fusion | flops 15727616 | bytes 81920 | tf_op jit(solution)/shard_map/while/body/eval_jaxpr/reduce_sum | solution.py:43
  59.5 4.2 %all-to-all-start.1 = ((f32[9,16,256]{2,0,1:T(8,128)}), f32[9,16,256]{2,0,1:T(8,128)S(1)}, u32[]{:S(2)}, u32[]{:S(2)}) async-start(f32[9,16,256]{2,0,1:T(8,128)} %multiply_bitcast_fusion), calls=%async_computation.1 | async-start | bytes 524288 | tf_op jit(solution)/shard_map/all_to_all | solution.py:118
  63.7 3.5 %collective-permute-start.2 = (f32[9,4,256]{2,0,1:T(8,128)S(1)}, f32[9,4,256]{2,0,1:T(8,128)S(1)}, u32[]{:S(2)}, u32[]{:S(2)}) collective-permute-start(f32[9,4,256]{2,0,1:T(8,128)S(1)} %get-tuple-element.202), channel_id=1, source_target_pairs={{0,8},{8,16},{16,24},{1,9},{9,17},{17,25},{2,10},{10,18},{18,26},{... | collective-permute-start | bytes 110600 | tf_op jit(solution)/shard_map/ppermute | solution.py:25
  67.2 1.3 collective-permute-start.3
  69.2 4.2 %collective-permute-done.3 = f32[9,4,256]{2,0,1:T(8,128)S(1)} collective-permute-done((f32[9,4,256]{2,0,1:T(8,128)S(1)}, f32[9,4,256]{2,0,1:T(8,128)S(1)}, u32[]{:S(2)}, u32[]{:S(2)}) %collective-permute-start.3) | collective-permute-done | bytes 36896 | tf_op jit(solution)/shard_map/ppermute | solution.py:27
  73.5 81.7 %while.21 = (s32[]{:T(128)}, f32[8,3,4,256]{3,1,2,0:T(4,128)S(1)}, s32[8,4]{1,0:T(8,128)S(1)}, f32[3,32,256]{2,0,1:T(4,128)S(1)}, s32[32,3]{1,0:T(8,128)S(1)}, /...) while((s32[]{:T(128)}, f32[8,3,4,256]{3,1,2,0:T(4,128)S(1)}, ...), condition=%wide.region_12.13_spmd, body=%wide.region_7.12_spmd.sunk | while | flops 35666000 | bytes 1299173 | solution.py:131
  76.3 6.7 %fusion.61 = (f32[4,256]{1,0:T(4,128)S(1)}, f32[4,256]{1,0:T(4,128)S(1)}, f32[4,256]{1,0:T(4,128)S(1)}, f32[4,256]{1,0:T(4,128)S(1)}) fusion(f32[4,4,256]{2,1,0:T(4,128)S(1)} %get-tuple-element.362, f32[4,4,256]{2,1,0:T(4,128)S(1)} %bitcast.193, f32[4,256]{1,0:T(4,128)S(1)} %bitcast.198, f32[4,4,256]{2,1,0:T(4,128)S(1)} %get-tuple-element.367, ...), kind=kLoop, calls=%fused_computation.45.clone.1 | loop fusion | flops 35647488 | bytes 196608 | tf_op jit(solution)/shard_map/while/body/eval_jaxpr/reduce_sum | solution.py:71
  86.5 6.7 %fusion.61 = (f32[4,256]{1,0:T(4,128)S(1)}, f32[4,256]{1,0:T(4,128)S(1)}, f32[4,256]{1,0:T(4,128)S(1)}, f32[4,256]{1,0:T(4,128)S(1)}) fusion(f32[4,4,256]{2,1,0:T(4,128)S(1)} %get-tuple-element.362, f32[4,4,256]{2,1,0:T(4,128)S(1)} %bitcast.193, f32[4,256]{1,0:T(4,128)S(1)} %bitcast.198, f32[4,4,256]{2,1,0:T(4,128)S(1)} %get-tuple-element.367, ...), kind=kLoop, calls=%fused_computation.45.clone.1 | loop fusion | flops 35647488 | bytes 196608 | tf_op jit(solution)/shard_map/while/body/eval_jaxpr/reduce_sum | solution.py:71
  96.7 6.7 %fusion.61 = (f32[4,256]{1,0:T(4,128)S(1)}, f32[4,256]{1,0:T(4,128)S(1)}, f32[4,256]{1,0:T(4,128)S(1)}, f32[4,256]{1,0:T(4,128)S(1)}) fusion(f32[4,4,256]{2,1,0:T(4,128)S(1)} %get-tuple-element.362, f32[4,4,256]{2,1,0:T(4,128)S(1)} %bitcast.193, f32[4,256]{1,0:T(4,128)S(1)} %bitcast.198, f32[4,4,256]{2,1,0:T(4,128)S(1)} %get-tuple-element.367, ...), kind=kLoop, calls=%fused_computation.45.clone.1 | loop fusion | flops 35647488 | bytes 196608 | tf_op jit(solution)/shard_map/while/body/eval_jaxpr/reduce_sum | solution.py:71
  106.9 6.7 %fusion.61 = (f32[4,256]{1,0:T(4,128)S(1)}, f32[4,256]{1,0:T(4,128)S(1)}, f32[4,256]{1,0:T(4,128)S(1)}, f32[4,256]{1,0:T(4,128)S(1)}) fusion(f32[4,4,256]{2,1,0:T(4,128)S(1)} %get-tuple-element.362, f32[4,4,256]{2,1,0:T(4,128)S(1)} %bitcast.193, f32[4,256]{1,0:T(4,128)S(1)} %bitcast.198, f32[4,4,256]{2,1,0:T(4,128)S(1)} %get-tuple-element.367, ...), kind=kLoop, calls=%fused_computation.45.clone.1 | loop fusion | flops 35647488 | bytes 196608 | tf_op jit(solution)/shard_map/while/body/eval_jaxpr/reduce_sum | solution.py:71
  117.2 6.7 %fusion.61 = (f32[4,256]{1,0:T(4,128)S(1)}, f32[4,256]{1,0:T(4,128)S(1)}, f32[4,256]{1,0:T(4,128)S(1)}, f32[4,256]{1,0:T(4,128)S(1)}) fusion(f32[4,4,256]{2,1,0:T(4,128)S(1)} %get-tuple-element.362, f32[4,4,256]{2,1,0:T(4,128)S(1)} %bitcast.193, f32[4,256]{1,0:T(4,128)S(1)} %bitcast.198, f32[4,4,256]{2,1,0:T(4,128)S(1)} %get-tuple-element.367, ...), kind=kLoop, calls=%fused_computation.45.clone.1 | loop fusion | flops 35647488 | bytes 196608 | tf_op jit(solution)/shard_map/while/body/eval_jaxpr/reduce_sum | solution.py:71
  127.4 6.7 %fusion.61 = (f32[4,256]{1,0:T(4,128)S(1)}, f32[4,256]{1,0:T(4,128)S(1)}, f32[4,256]{1,0:T(4,128)S(1)}, f32[4,256]{1,0:T(4,128)S(1)}) fusion(f32[4,4,256]{2,1,0:T(4,128)S(1)} %get-tuple-element.362, f32[4,4,256]{2,1,0:T(4,128)S(1)} %bitcast.193, f32[4,256]{1,0:T(4,128)S(1)} %bitcast.198, f32[4,4,256]{2,1,0:T(4,128)S(1)} %get-tuple-element.367, ...), kind=kLoop, calls=%fused_computation.45.clone.1 | loop fusion | flops 35647488 | bytes 196608 | tf_op jit(solution)/shard_map/while/body/eval_jaxpr/reduce_sum | solution.py:71
  137.6 6.7 %fusion.61 = (f32[4,256]{1,0:T(4,128)S(1)}, f32[4,256]{1,0:T(4,128)S(1)}, f32[4,256]{1,0:T(4,128)S(1)}, f32[4,256]{1,0:T(4,128)S(1)}) fusion(f32[4,4,256]{2,1,0:T(4,128)S(1)} %get-tuple-element.362, f32[4,4,256]{2,1,0:T(4,128)S(1)} %bitcast.193, f32[4,256]{1,0:T(4,128)S(1)} %bitcast.198, f32[4,4,256]{2,1,0:T(4,128)S(1)} %get-tuple-element.367, ...), kind=kLoop, calls=%fused_computation.45.clone.1 | loop fusion | flops 35647488 | bytes 196608 | tf_op jit(solution)/shard_map/while/body/eval_jaxpr/reduce_sum | solution.py:71
  147.8 6.7 %fusion.61 = (f32[4,256]{1,0:T(4,128)S(1)}, f32[4,256]{1,0:T(4,128)S(1)}, f32[4,256]{1,0:T(4,128)S(1)}, f32[4,256]{1,0:T(4,128)S(1)}) fusion(f32[4,4,256]{2,1,0:T(4,128)S(1)} %get-tuple-element.362, f32[4,4,256]{2,1,0:T(4,128)S(1)} %bitcast.193, f32[4,256]{1,0:T(4,128)S(1)} %bitcast.198, f32[4,4,256]{2,1,0:T(4,128)S(1)} %get-tuple-element.367, ...), kind=kLoop, calls=%fused_computation.45.clone.1 | loop fusion | flops 35647488 | bytes 196608 | tf_op jit(solution)/shard_map/while/body/eval_jaxpr/reduce_sum | solution.py:71
  156.2 4.3 %scatter_fusion = f32[7,16,256]{2,0,1:T(8,128)} fusion(f32[7,16,256]{2,0,1:T(8,128)} %broadcast_in_dim.48, s32[32]{0:T(128)S(1)} %get-tuple-element.210, f32[32,7,256]{2,1,0:T(8,128)S(1)} %copy.53), kind=kCustom, calls=%fused_computation.10 | custom fusion | bytes 688256 | tf_op jit(solution)/shard_map/scatter | solution.py:151
  160.5 4.2 %all-to-all-start.2 = ((f32[7,16,256]{2,0,1:T(8,128)}), f32[7,16,256]{2,0,1:T(8,128)S(1)}, u32[]{:S(2)}, u32[]{:S(2)}) async-start(f32[7,16,256]{2,0,1:T(8,128)} %scatter_fusion), calls=%async_computation.2 | async-start | bytes 262144 | tf_op jit(solution)/shard_map/all_to_all | solution.py:153
  164.7 5.5 %all-to-all-done.2 = f32[7,16,256]{2,0,1:T(8,128)S(1)} async-done(((f32[7,16,256]{2,0,1:T(8,128)}), f32[7,16,256]{2,0,1:T(8,128)S(1)}, u32[]{:S(2)}, u32[]{:S(2)}) %all-to-all-start.2) | async-done | bytes 114720 | tf_op jit(solution)/shard_map/all_to_all | solution.py:153
  170.2 1.0 scatter_fusion.1
  171.3 1.5 scatter_fusion.2
  (382 shorter events, 55.1 us)
Async XLA Ops:
  0.6 15.0 %copy-start.2 = (s32[32]{0:T(128)S(1)}, s32[32]{0:T(128)}, u32[]{:S(2)}) copy-start(s32[32]{0:T(128)} %param.16) | copy-start | bytes 388
  0.6 15.1 %copy-start.3 = (s32[1,256]{1,0:T(1,128)S(1)}, s32[1,256]{1,0:T(1,128)}, u32[]{:S(2)}) copy-start(s32[1,256]{1,0:T(1,128)} %param.20) | copy-start | bytes 3076
  0.7 17.3 %copy-start.4 = (s32[32,3]{0,1:T(4,128)S(1)}, s32[32,3]{0,1:T(4,128)}, u32[]{:S(2)}) copy-start(s32[32,3]{0,1:T(4,128)} %param.18) | copy-start | bytes 1156
  0.7 17.4 %copy-start.1 = (f32[3,32,256]{2,1,0:T(8,128)S(1)}, f32[3,32,256]{2,1,0:T(8,128)}, u32[]{:S(2)}) copy-start(f32[3,32,256]{2,1,0:T(8,128)} %param.14) | copy-start | bytes 294916
  5.7 14.3 %all-to-all-start = ((f32[4,16,256]{2,0,1:T(4,128)}), f32[4,16,256]{2,0,1:T(4,128)S(1)}, u32[]{:S(2)}, u32[]{:S(2)}) async-start(f32[4,16,256]{2,0,1:T(4,128)} %multiply_bitcast_fusion.1), calls=%async_computation | async-start | bytes 131072 | tf_op jit(solution)/shard_map/all_to_all | solution.py:102
  10.9 7.4 %collective-permute-start = (f32[4,4,256]{2,0,1:T(4,128)S(1)}, f32[4,4,256]{2,0,1:T(4,128)S(1)}, u32[]{:S(2)}, u32[]{:S(2)}) collective-permute-start(f32[4,4,256]{2,0,1:T(4,128)S(1)} %get-tuple-element.204), channel_id=1, source_target_pairs={{0,8},{8,16},{16,24},{1,9},{9,17},{17,25},{2,10},{10,18},{18,26},{... | collective-permute-start | bytes 49160 | tf_op jit(solution)/shard_map/ppermute | solution.py:25
  14.4 5.6 %collective-permute-start.1 = (f32[4,4,256]{2,0,1:T(4,128)S(1)}, f32[4,4,256]{2,0,1:T(4,128)S(1)}, u32[]{:S(2)}, u32[]{:S(2)}) collective-permute-start(f32[4,4,256]{2,0,1:T(4,128)S(1)} %get-tuple-element.205), channel_id=1, source_target_pairs={{8,0},{16,8},{24,16},{9,1},{17,9},{25,17},{10,2},{18,10},{26,18},{... | collective-permute-start | bytes 49160 | tf_op jit(solution)/shard_map/ppermute | solution.py:27
  59.5 13.8 %all-to-all-start.1 = ((f32[9,16,256]{2,0,1:T(8,128)}), f32[9,16,256]{2,0,1:T(8,128)S(1)}, u32[]{:S(2)}, u32[]{:S(2)}) async-start(f32[9,16,256]{2,0,1:T(8,128)} %multiply_bitcast_fusion), calls=%async_computation.1 | async-start | bytes 524288 | tf_op jit(solution)/shard_map/all_to_all | solution.py:118
  63.7 5.5 %collective-permute-start.2 = (f32[9,4,256]{2,0,1:T(8,128)S(1)}, f32[9,4,256]{2,0,1:T(8,128)S(1)}, u32[]{:S(2)}, u32[]{:S(2)}) collective-permute-start(f32[9,4,256]{2,0,1:T(8,128)S(1)} %get-tuple-element.202), channel_id=1, source_target_pairs={{0,8},{8,16},{16,24},{1,9},{9,17},{17,25},{2,10},{10,18},{18,26},{... | collective-permute-start | bytes 110600 | tf_op jit(solution)/shard_map/ppermute | solution.py:25
  67.2 6.2 %collective-permute-start.3 = (f32[9,4,256]{2,0,1:T(8,128)S(1)}, f32[9,4,256]{2,0,1:T(8,128)S(1)}, u32[]{:S(2)}, u32[]{:S(2)}) collective-permute-start(f32[9,4,256]{2,0,1:T(8,128)S(1)} %get-tuple-element.203), channel_id=1, source_target_pairs={{8,0},{16,8},{24,16},{9,1},{17,9},{25,17},{10,2},{18,10},{26,18},{... | collective-permute-start | bytes 110600 | tf_op jit(solution)/shard_map/ppermute | solution.py:27
  73.4 81.8 %copy-start = (f32[3,32,256]{2,1,0:T(8,128)S(1)}, f32[3,32,256]{2,1,0:T(8,128)}, u32[]{:S(2)}) copy-start(f32[3,32,256]{2,1,0:T(8,128)} %param.13) | copy-start | bytes 294916
  73.4 81.8 %copy-start.5 = (f32[3]{0:T(128)S(1)}, f32[3]{0:T(128)}, u32[]{:S(2)}) copy-start(f32[3]{0:T(128)} %constant.111) | copy-start | bytes 40
  160.5 9.7 %all-to-all-start.2 = ((f32[7,16,256]{2,0,1:T(8,128)}), f32[7,16,256]{2,0,1:T(8,128)S(1)}, u32[]{:S(2)}, u32[]{:S(2)}) async-start(f32[7,16,256]{2,0,1:T(8,128)} %scatter_fusion), calls=%async_computation.2 | async-start | bytes 262144 | tf_op jit(solution)/shard_map/all_to_all | solution.py:153
where the time goes:
time: 175 us; the launch traced here: 174 us
  other arithmetic  81.9 us (47%)
  local copies, waits for them, and re-layouts  54.5 us (31%)
  starting transfers between devices  23.1 us (13%)
  waiting for transfers between devices  12 us (7%)
  loops' own time  1.75 us (1%)
    reduce_sum x8, other arithmetic, pair_force(): jnp.sum(offsets[component] * pushes + damping * remote[3 + component][:,...  54 us
    reduce_sum x8, other arithmetic, pair_density(): jnp.sum(remote[3][:, None, :, :] * weight * weight * weight, axis=(2, 3))  20 us
    ppermute x2, starting transfers between devices, with_halo(): lax.ppermute(tail, axis, [(i, (i + 1) % count) for i in range(ends)])  6.96 us
    ppermute x2, waiting for transfers between devices, with_halo(): lax.ppermute(head, axis, [((i + 1) % count, i) for i in range(ends)])  5.9 us
    all_to_all x1, waiting for transfers between devices, shards(): lax.all_to_all(outbox, 'dev', split_axis=1, concat_axis=1, tiled=True)  5.49 us
    all_to_all x1, starting transfers between devices, shards(): lax.all_to_all(outgoing(dens_field), 'dev', split_axis=1, concat_axis=1,...  5.2 us
    gather x8, local copies, waits for them, and re-layouts, pair_density(): remote = lookup[:, columns, :]  4.75 us
    gather x8, local copies, waits for them, and re-layouts, force_block(): velocities[:, cell_ids, :]  4.59 us
  transfers between devices with their start and end apart: 7, of which 4 were waited for; matrix products, arithmetic and copies ran while one was open for 2% of the time, Pallas kernels for 0%

commit v1 on v0

--- a/solution.py
+++ b/solution.py
@@ -150,7 +150,18 @@
         .at[:, slot_index, :]
         .set(moved, mode="drop")
     )
-    inbox = lax.all_to_all(outbox, "dev", split_axis=1, concat_axis=1, tiled=True)
+    ways, here = (lax.axis_size("dev"), lax.axis_index("dev"))
+    width_2 = outbox.shape[1] // ways
+    shape = list(outbox.shape)
+    shape[1] = width_2
+    height = shape[1]
+    shape[1] = height * ways
+    inbox = jnp.zeros(shape, outbox.dtype)
+    for mask in range(ways):
+        part = lax.dynamic_slice_in_dim(outbox, (here ^ mask) * width_2, width_2, axis=1)
+        if mask:
+            part = lax.ppermute(part, "dev", [(d, d ^ mask) for d in range(ways)])
+        inbox = lax.dynamic_update_slice_in_dim(inbox, part, (here ^ mask) * height, axis=1)
     arrivals = jnp.sum(
         (group_owner.reshape(peer_count, cell_count) == own_index).astype(jnp.int32), 1
     )

time: 175 us -> 172 us (0.983)
  local copies, waits for them, and re-layouts: 54.5 us -> 51.1 us
  starting transfers between devices: 23.1 us -> 25.6 us
    ppermute x0 -> x7, starting transfers between devices: none -> 6.66 us  [shards(): part = lax.ppermute(part, 'dev', [(d, d ^ mask) for d in range(ways)])]
    all_to_all x1 -> x0, waiting for transfers between devices: 5.49 us -> none  [shards(): lax.all_to_all(outbox, 'dev', split_axis=1, concat_axis=1, tiled=True)]
    all_to_all x1 -> x0, starting transfers between devices: 4.18 us -> none  [shards(): lax.all_to_all(outbox, 'dev', split_axis=1, concat_axis=1, tiled=True)]
    ppermute x0 -> x7, waiting for transfers between devices: none -> 3.92 us  [shards(): part = lax.ppermute(part, 'dev', [(d, d ^ mask) for d in range(ways)])]
    scatter x1, local copies, waits for them, and re-layouts: 4.34 us -> 1.56 us  [shards(): outbox = jnp.zeros((7, peer_count * capacity, block_width), jnp.float32)....]
  transfers between devices with their start and end apart: 7 -> 13, of which waited for: 4 -> 6; matrix products, arithmetic and copies ran while one was open for 2% -> 2% of each run, Pallas kernels for 0% -> 0%
where the time goes in v1:
time: 172 us
  other arithmetic  81.9 us (48%)
  local copies, waits for them, and re-layouts  51.1 us (30%)
  starting transfers between devices  25.6 us (15%)
  waiting for transfers between devices  10.4 us (6%)
  loops' own time  1.75 us (1%)
    reduce_sum x8, other arithmetic, pair_force(): jnp.sum(offsets[component] * pushes + damping * remote[3 + component][:,...  54 us
    reduce_sum x8, other arithmetic, pair_density(): jnp.sum(remote[3][:, None, :, :] * weight * weight * weight, axis=(2, 3))  20 us
    ppermute x2, starting transfers between devices, with_halo(): lax.ppermute(tail, axis, [(i, (i + 1) % count) for i in range(ends)])  6.96 us
    ppermute x7, starting transfers between devices, shards(): part = lax.ppermute(part, 'dev', [(d, d ^ mask) for d in range(ways)])  6.66 us
    ppermute x2, waiting for transfers between devices, with_halo(): lax.ppermute(head, axis, [((i + 1) % count, i) for i in range(ends)])  5.83 us
    all_to_all x1, starting transfers between devices, shards(): lax.all_to_all(outgoing(dens_field), 'dev', split_axis=1, concat_axis=1,...  5.2 us
    gather x8, local copies, waits for them, and re-layouts, pair_density(): remote = lookup[:, columns, :]  4.75 us
    gather x8, local copies, waits for them, and re-layouts, force_block(): velocities[:, cell_ids, :]  4.59 us
  transfers between devices with their start and end apart: 13, of which 6 were waited for; matrix products, arithmetic and copies ran while one was open for 2% of the time, Pallas kernels for 0%

profile of v1, /device:TPU:0, one launch (start us, length us, event | category | flops | bytes accessed | tf_op | source)
XLA Modules:
  0.0 171.8 jit_solution(12682704590440829815)
XLA Ops:
  5.7 5.2 %all-to-all-start = ((f32[4,16,256]{2,0,1:T(4,128)}), f32[4,16,256]{2,0,1:T(4,128)S(1)}, u32[]{:S(2)}, u32[]{:S(2)}) async-start(f32[4,16,256]{2,0,1:T(4,128)} %multiply_bitcast_fusion.1), calls=%async_computation | async-start | bytes 131072 | tf_op jit(solution)/shard_map/all_to_all | solution.py:102
  10.9 3.5 %collective-permute-start = (f32[4,4,256]{2,0,1:T(4,128)S(1)}, f32[4,4,256]{2,0,1:T(4,128)S(1)}, u32[]{:S(2)}, u32[]{:S(2)}) collective-permute-start(f32[4,4,256]{2,0,1:T(4,128)S(1)} %get-tuple-element.204), channel_id=1, source_target_pairs={{0,8},{8,16},{16,24},{1,9},{9,17},{17,25},{2,10},{10,18},{18,26},{... | collective-permute-start | bytes 49160 | tf_op jit(solution)/shard_map/ppermute | solution.py:25
  18.3 1.7 collective-permute-done.1
  20.1 37.5 %while.20 = (s32[]{:T(128)}, f32[8,4,256]{2,1,0:T(4,128)S(1)}, s32[8,4]{1,0:T(8,128)S(1)}, s32[32,3]{1,0:T(8,128)S(1)}, f32[4,56,256]{2,0,1:T(4,128)S(1)}, /*index=5*/f32[3,32,256]{2,0,1:T(4,128)S(1)}, s32[]{:T(128)}) while((s32[]{:T(128)}, f32[8,4,256]{2,1,0:T(4,128)S(1)}, s32[8,4]{1,0:T(8,128)S(1)}, s32[32,3]{1,0:T(8,128)S(1)}, ...), condition=%wide.region_6.7_spmd, body=%wide.region_4.0_spmd.sunk | while | flops 15729746 | bytes 565941 | solution.py:110
  22.3 2.5 %fusion.57 = f32[4,256]{1,0:T(4,128)S(1)} fusion(f32[4,4,256]{2,1,0:T(4,128)S(1)} %get-tuple-element.347, f32[4,256]{1,0:T(4,128)S(1)} %get-tuple-element.350, f32[4,4,256]{2,1,0:T(4,128)S(1)} %get-tuple-element.351, f32[4,256]{1,0:T(4,128)S(1)} %get-tuple-element.352, f32[4,4,256]{2,1,0:T(4,128)S(1)} %get-tuple-element.355, ...), kind=kLoop, calls=%fused_computation.14.clone.1 | loop fusion | flops 15727616 | bytes 81920 | tf_op jit(solution)/shard_map/while/body/eval_jaxpr/reduce_sum | solution.py:43
  27.0 2.5 %fusion.57 = f32[4,256]{1,0:T(4,128)S(1)} fusion(f32[4,4,256]{2,1,0:T(4,128)S(1)} %get-tuple-element.347, f32[4,256]{1,0:T(4,128)S(1)} %get-tuple-element.350, f32[4,4,256]{2,1,0:T(4,128)S(1)} %get-tuple-element.351, f32[4,256]{1,0:T(4,128)S(1)} %get-tuple-element.352, f32[4,4,256]{2,1,0:T(4,128)S(1)} %get-tuple-element.355, ...), kind=kLoop, calls=%fused_computation.14.clone.1 | loop fusion | flops 15727616 | bytes 81920 | tf_op jit(solution)/shard_map/while/body/eval_jaxpr/reduce_sum | solution.py:43
  31.7 2.5 %fusion.57 = f32[4,256]{1,0:T(4,128)S(1)} fusion(f32[4,4,256]{2,1,0:T(4,128)S(1)} %get-tuple-element.347, f32[4,256]{1,0:T(4,128)S(1)} %get-tuple-element.350, f32[4,4,256]{2,1,0:T(4,128)S(1)} %get-tuple-element.351, f32[4,256]{1,0:T(4,128)S(1)} %get-tuple-element.352, f32[4,4,256]{2,1,0:T(4,128)S(1)} %get-tuple-element.355, ...), kind=kLoop, calls=%fused_computation.14.clone.1 | loop fusion | flops 15727616 | bytes 81920 | tf_op jit(solution)/shard_map/while/body/eval_jaxpr/reduce_sum | solution.py:43
  36.3 2.5 %fusion.57 = f32[4,256]{1,0:T(4,128)S(1)} fusion(f32[4,4,256]{2,1,0:T(4,128)S(1)} %get-tuple-element.347, f32[4,256]{1,0:T(4,128)S(1)} %get-tuple-element.350, f32[4,4,256]{2,1,0:T(4,128)S(1)} %get-tuple-element.351, f32[4,256]{1,0:T(4,128)S(1)} %get-tuple-element.352, f32[4,4,256]{2,1,0:T(4,128)S(1)} %get-tuple-element.355, ...), kind=kLoop, calls=%fused_computation.14.clone.1 | loop fusion | flops 15727616 | bytes 81920 | tf_op jit(solution)/shard_map/while/body/eval_jaxpr/reduce_sum | solution.py:43
  41.0 2.5 %fusion.57 = f32[4,256]{1,0:T(4,128)S(1)} fusion(f32[4,4,256]{2,1,0:T(4,128)S(1)} %get-tuple-element.347, f32[4,256]{1,0:T(4,128)S(1)} %get-tuple-element.350, f32[4,4,256]{2,1,0:T(4,128)S(1)} %get-tuple-element.351, f32[4,256]{1,0:T(4,128)S(1)} %get-tuple-element.352, f32[4,4,256]{2,1,0:T(4,128)S(1)} %get-tuple-element.355, ...), kind=kLoop, calls=%fused_computation.14.clone.1 | loop fusion | flops 15727616 | bytes 81920 | tf_op jit(solution)/shard_map/while/body/eval_jaxpr/reduce_sum | solution.py:43
  45.7 2.5 %fusion.57 = f32[4,256]{1,0:T(4,128)S(1)} fusion(f32[4,4,256]{2,1,0:T(4,128)S(1)} %get-tuple-element.347, f32[4,256]{1,0:T(4,128)S(1)} %get-tuple-element.350, f32[4,4,256]{2,1,0:T(4,128)S(1)} %get-tuple-element.351, f32[4,256]{1,0:T(4,128)S(1)} %get-tuple-element.352, f32[4,4,256]{2,1,0:T(4,128)S(1)} %get-tuple-element.355, ...), kind=kLoop, calls=%fused_computation.14.clone.1 | loop fusion | flops 15727616 | bytes 81920 | tf_op jit(solution)/shard_map/while/body/eval_jaxpr/reduce_sum | solution.py:43
  50.4 2.5 %fusion.57 = f32[4,256]{1,0:T(4,128)S(1)} fusion(f32[4,4,256]{2,1,0:T(4,128)S(1)} %get-tuple-element.347, f32[4,256]{1,0:T(4,128)S(1)} %get-tuple-element.350, f32[4,4,256]{2,1,0:T(4,128)S(1)} %get-tuple-element.351, f32[4,256]{1,0:T(4,128)S(1)} %get-tuple-element.352, f32[4,4,256]{2,1,0:T(4,128)S(1)} %get-tuple-element.355, ...), kind=kLoop, calls=%fused_computation.14.clone.1 | loop fusion | flops 15727616 | bytes 81920 | tf_op jit(solution)/shard_map/while/body/eval_jaxpr/reduce_sum | solution.py:43
  55.1 2.5 %fusion.57 = f32[4,256]{1,0:T(4,128)S(1)} fusion(f32[4,4,256]{2,1,0:T(4,128)S(1)} %get-tuple-element.347, f32[4,256]{1,0:T(4,128)S(1)} %get-tuple-element.350, f32[4,4,256]{2,1,0:T(4,128)S(1)} %get-tuple-element.351, f32[4,256]{1,0:T(4,128)S(1)} %get-tuple-element.352, f32[4,4,256]{2,1,0:T(4,128)S(1)} %get-tuple-element.355, ...), kind=kLoop, calls=%fused_computation.14.clone.1 | loop fusion | flops 15727616 | bytes 81920 | tf_op jit(solution)/shard_map/while/body/eval_jaxpr/reduce_sum | solution.py:43
  59.5 4.2 %all-to-all-start.1 = ((f32[9,16,256]{2,0,1:T(8,128)}), f32[9,16,256]{2,0,1:T(8,128)S(1)}, u32[]{:S(2)}, u32[]{:S(2)}) async-start(f32[9,16,256]{2,0,1:T(8,128)} %multiply_bitcast_fusion), calls=%async_computation.1 | async-start | bytes 524288 | tf_op jit(solution)/shard_map/all_to_all | solution.py:118
  63.7 3.5 %collective-permute-start.2 = (f32[9,4,256]{2,0,1:T(8,128)S(1)}, f32[9,4,256]{2,0,1:T(8,128)S(1)}, u32[]{:S(2)}, u32[]{:S(2)}) collective-permute-start(f32[9,4,256]{2,0,1:T(8,128)S(1)} %get-tuple-element.202), channel_id=1, source_target_pairs={{0,8},{8,16},{16,24},{1,9},{9,17},{17,25},{2,10},{10,18},{18,26},{... | collective-permute-start | bytes 110600 | tf_op jit(solution)/shard_map/ppermute | solution.py:25
  67.2 1.3 collective-permute-start.3
  69.2 4.2 %collective-permute-done.3 = f32[9,4,256]{2,0,1:T(8,128)S(1)} collective-permute-done((f32[9,4,256]{2,0,1:T(8,128)S(1)}, f32[9,4,256]{2,0,1:T(8,128)S(1)}, u32[]{:S(2)}, u32[]{:S(2)}) %collective-permute-start.3) | collective-permute-done | bytes 36896 | tf_op jit(solution)/shard_map/ppermute | solution.py:27
  73.5 81.7 %while.21 = (s32[]{:T(128)}, f32[8,3,4,256]{3,1,2,0:T(4,128)S(1)}, s32[8,4]{1,0:T(8,128)S(1)}, f32[3,32,256]{2,0,1:T(4,128)S(1)}, s32[32,3]{1,0:T(8,128)S(1)}, /...) while((s32[]{:T(128)}, f32[8,3,4,256]{3,1,2,0:T(4,128)S(1)}, ...), condition=%wide.region_12.13_spmd, body=%wide.region_7.12_spmd.sunk | while | flops 35666000 | bytes 1299173 | solution.py:131
  76.3 6.7 %fusion.61 = (f32[4,256]{1,0:T(4,128)S(1)}, f32[4,256]{1,0:T(4,128)S(1)}, f32[4,256]{1,0:T(4,128)S(1)}, f32[4,256]{1,0:T(4,128)S(1)}) fusion(f32[4,4,256]{2,1,0:T(4,128)S(1)} %get-tuple-element.370, f32[4,4,256]{2,1,0:T(4,128)S(1)} %bitcast.193, f32[4,256]{1,0:T(4,128)S(1)} %bitcast.198, f32[4,4,256]{2,1,0:T(4,128)S(1)} %get-tuple-element.375, ...), kind=kLoop, calls=%fused_computation.45.clone.1 | loop fusion | flops 35647488 | bytes 196608 | tf_op jit(solution)/shard_map/while/body/eval_jaxpr/reduce_sum | solution.py:71
  86.5 6.7 %fusion.61 = (f32[4,256]{1,0:T(4,128)S(1)}, f32[4,256]{1,0:T(4,128)S(1)}, f32[4,256]{1,0:T(4,128)S(1)}, f32[4,256]{1,0:T(4,128)S(1)}) fusion(f32[4,4,256]{2,1,0:T(4,128)S(1)} %get-tuple-element.370, f32[4,4,256]{2,1,0:T(4,128)S(1)} %bitcast.193, f32[4,256]{1,0:T(4,128)S(1)} %bitcast.198, f32[4,4,256]{2,1,0:T(4,128)S(1)} %get-tuple-element.375, ...), kind=kLoop, calls=%fused_computation.45.clone.1 | loop fusion | flops 35647488 | bytes 196608 | tf_op jit(solution)/shard_map/while/body/eval_jaxpr/reduce_sum | solution.py:71
  96.7 6.7 %fusion.61 = (f32[4,256]{1,0:T(4,128)S(1)}, f32[4,256]{1,0:T(4,128)S(1)}, f32[4,256]{1,0:T(4,128)S(1)}, f32[4,256]{1,0:T(4,128)S(1)}) fusion(f32[4,4,256]{2,1,0:T(4,128)S(1)} %get-tuple-element.370, f32[4,4,256]{2,1,0:T(4,128)S(1)} %bitcast.193, f32[4,256]{1,0:T(4,128)S(1)} %bitcast.198, f32[4,4,256]{2,1,0:T(4,128)S(1)} %get-tuple-element.375, ...), kind=kLoop, calls=%fused_computation.45.clone.1 | loop fusion | flops 35647488 | bytes 196608 | tf_op jit(solution)/shard_map/while/body/eval_jaxpr/reduce_sum | solution.py:71
  106.9 6.7 %fusion.61 = (f32[4,256]{1,0:T(4,128)S(1)}, f32[4,256]{1,0:T(4,128)S(1)}, f32[4,256]{1,0:T(4,128)S(1)}, f32[4,256]{1,0:T(4,128)S(1)}) fusion(f32[4,4,256]{2,1,0:T(4,128)S(1)} %get-tuple-element.370, f32[4,4,256]{2,1,0:T(4,128)S(1)} %bitcast.193, f32[4,256]{1,0:T(4,128)S(1)} %bitcast.198, f32[4,4,256]{2,1,0:T(4,128)S(1)} %get-tuple-element.375, ...), kind=kLoop, calls=%fused_computation.45.clone.1 | loop fusion | flops 35647488 | bytes 196608 | tf_op jit(solution)/shard_map/while/body/eval_jaxpr/reduce_sum | solution.py:71
  117.2 6.7 %fusion.61 = (f32[4,256]{1,0:T(4,128)S(1)}, f32[4,256]{1,0:T(4,128)S(1)}, f32[4,256]{1,0:T(4,128)S(1)}, f32[4,256]{1,0:T(4,128)S(1)}) fusion(f32[4,4,256]{2,1,0:T(4,128)S(1)} %get-tuple-element.370, f32[4,4,256]{2,1,0:T(4,128)S(1)} %bitcast.193, f32[4,256]{1,0:T(4,128)S(1)} %bitcast.198, f32[4,4,256]{2,1,0:T(4,128)S(1)} %get-tuple-element.375, ...), kind=kLoop, calls=%fused_computation.45.clone.1 | loop fusion | flops 35647488 | bytes 196608 | tf_op jit(solution)/shard_map/while/body/eval_jaxpr/reduce_sum | solution.py:71
  127.4 6.7 %fusion.61 = (f32[4,256]{1,0:T(4,128)S(1)}, f32[4,256]{1,0:T(4,128)S(1)}, f32[4,256]{1,0:T(4,128)S(1)}, f32[4,256]{1,0:T(4,128)S(1)}) fusion(f32[4,4,256]{2,1,0:T(4,128)S(1)} %get-tuple-element.370, f32[4,4,256]{2,1,0:T(4,128)S(1)} %bitcast.193, f32[4,256]{1,0:T(4,128)S(1)} %bitcast.198, f32[4,4,256]{2,1,0:T(4,128)S(1)} %get-tuple-element.375, ...), kind=kLoop, calls=%fused_computation.45.clone.1 | loop fusion | flops 35647488 | bytes 196608 | tf_op jit(solution)/shard_map/while/body/eval_jaxpr/reduce_sum | solution.py:71
  137.6 6.7 %fusion.61 = (f32[4,256]{1,0:T(4,128)S(1)}, f32[4,256]{1,0:T(4,128)S(1)}, f32[4,256]{1,0:T(4,128)S(1)}, f32[4,256]{1,0:T(4,128)S(1)}) fusion(f32[4,4,256]{2,1,0:T(4,128)S(1)} %get-tuple-element.370, f32[4,4,256]{2,1,0:T(4,128)S(1)} %bitcast.193, f32[4,256]{1,0:T(4,128)S(1)} %bitcast.198, f32[4,4,256]{2,1,0:T(4,128)S(1)} %get-tuple-element.375, ...), kind=kLoop, calls=%fused_computation.45.clone.1 | loop fusion | flops 35647488 | bytes 196608 | tf_op jit(solution)/shard_map/while/body/eval_jaxpr/reduce_sum | solution.py:71
  147.8 6.7 %fusion.61 = (f32[4,256]{1,0:T(4,128)S(1)}, f32[4,256]{1,0:T(4,128)S(1)}, f32[4,256]{1,0:T(4,128)S(1)}, f32[4,256]{1,0:T(4,128)S(1)}) fusion(f32[4,4,256]{2,1,0:T(4,128)S(1)} %get-tuple-element.370, f32[4,4,256]{2,1,0:T(4,128)S(1)} %bitcast.193, f32[4,256]{1,0:T(4,128)S(1)} %bitcast.198, f32[4,4,256]{2,1,0:T(4,128)S(1)} %get-tuple-element.375, ...), kind=kLoop, calls=%fused_computation.45.clone.1 | loop fusion | flops 35647488 | bytes 196608 | tf_op jit(solution)/shard_map/while/body/eval_jaxpr/reduce_sum | solution.py:71
  155.5 1.6 scatter_fusion
  157.2 2.1 %collective-permute-start.5 = (f32[7,2,256]{2,0,1:T(8,128)S(1)}, f32[7,2,256]{2,0,1:T(8,128)S(1)}, u32[]{:S(2)}, u32[]{:S(2)}) collective-permute-start(f32[7,2,256]{2,0,1:T(8,128)S(1)} %get-tuple-element.211), channel_id=1, source_target_pairs={{0,2},{1,3},{2,0},{3,1},{4,6},{5,7},{6,4},{7,5},{8,10},{9,11},{10,... | collective-permute-start | bytes 43016 | tf_op jit(solution)/shard_map/ppermute | solution.py:163
  159.4 1.7 %collective-permute-start.7 = (f32[7,2,256]{2,0,1:T(8,128)S(1)}, f32[7,2,256]{2,0,1:T(8,128)S(1)}, u32[]{:S(2)}, u32[]{:S(2)}) collective-permute-start(f32[7,2,256]{2,0,1:T(8,128)S(1)} %get-tuple-element.209), channel_id=1, source_target_pairs={{0,4},{1,5},{2,6},{3,7},{4,0},{5,1},{6,2},{7,3},{8,12},{9,13},{10,... | collective-permute-start | bytes 43016 | tf_op jit(solution)/shard_map/ppermute | solution.py:163
  161.1 2.6 %collective-permute-start.9 = (f32[7,2,256]{2,0,1:T(8,128)S(1)}, f32[7,2,256]{2,0,1:T(8,128)S(1)}, u32[]{:S(2)}, u32[]{:S(2)}) collective-permute-start(f32[7,2,256]{2,0,1:T(8,128)S(1)} %get-tuple-element.207), channel_id=1, source_target_pairs={{0,6},{1,7},{2,4},{3,5},{4,2},{5,3},{6,0},{7,1},{8,14},{9,15},{10,... | collective-permute-start | bytes 43016 | tf_op jit(solution)/shard_map/ppermute | solution.py:163
  164.3 1.5 collective-permute-done.9
  165.8 2.0 %collective-permute-done.10 = f32[7,2,256]{2,0,1:T(8,128)S(1)} collective-permute-done((f32[7,2,256]{2,0,1:T(8,128)S(1)}, f32[7,2,256]{2,0,1:T(8,128)S(1)}, u32[]{:S(2)}, u32[]{:S(2)}) %collective-permute-start.10) | collective-permute-done | bytes 14368 | tf_op jit(solution)/shard_map/ppermute | solution.py:163
  168.9 1.5 scatter_fusion.2
  (403 shorter events, 58.5 us)
Async XLA Ops:
  0.6 15.0 %copy-start.2 = (s32[32]{0:T(128)S(1)}, s32[32]{0:T(128)}, u32[]{:S(2)}) copy-start(s32[32]{0:T(128)} %param.16) | copy-start | bytes 388
  0.6 15.1 %copy-start.3 = (s32[1,256]{1,0:T(1,128)S(1)}, s32[1,256]{1,0:T(1,128)}, u32[]{:S(2)}) copy-start(s32[1,256]{1,0:T(1,128)} %param.20) | copy-start | bytes 3076
  0.7 17.4 %copy-start.4 = (s32[32,3]{0,1:T(4,128)S(1)}, s32[32,3]{0,1:T(4,128)}, u32[]{:S(2)}) copy-start(s32[32,3]{0,1:T(4,128)} %param.18) | copy-start | bytes 1156
  0.7 17.5 %copy-start.1 = (f32[3,32,256]{2,1,0:T(8,128)S(1)}, f32[3,32,256]{2,1,0:T(8,128)}, u32[]{:S(2)}) copy-start(f32[3,32,256]{2,1,0:T(8,128)} %param.14) | copy-start | bytes 294916
  5.7 14.3 %all-to-all-start = ((f32[4,16,256]{2,0,1:T(4,128)}), f32[4,16,256]{2,0,1:T(4,128)S(1)}, u32[]{:S(2)}, u32[]{:S(2)}) async-start(f32[4,16,256]{2,0,1:T(4,128)} %multiply_bitcast_fusion.1), calls=%async_computation | async-start | bytes 131072 | tf_op jit(solution)/shard_map/all_to_all | solution.py:102
  10.9 7.5 %collective-permute-start = (f32[4,4,256]{2,0,1:T(4,128)S(1)}, f32[4,4,256]{2,0,1:T(4,128)S(1)}, u32[]{:S(2)}, u32[]{:S(2)}) collective-permute-start(f32[4,4,256]{2,0,1:T(4,128)S(1)} %get-tuple-element.204), channel_id=1, source_target_pairs={{0,8},{8,16},{16,24},{1,9},{9,17},{17,25},{2,10},{10,18},{18,26},{... | collective-permute-start | bytes 49160 | tf_op jit(solution)/shard_map/ppermute | solution.py:25
  14.4 5.6 %collective-permute-start.1 = (f32[4,4,256]{2,0,1:T(4,128)S(1)}, f32[4,4,256]{2,0,1:T(4,128)S(1)}, u32[]{:S(2)}, u32[]{:S(2)}) collective-permute-start(f32[4,4,256]{2,0,1:T(4,128)S(1)} %get-tuple-element.205), channel_id=1, source_target_pairs={{8,0},{16,8},{24,16},{9,1},{17,9},{25,17},{10,2},{18,10},{26,18},{... | collective-permute-start | bytes 49160 | tf_op jit(solution)/shard_map/ppermute | solution.py:27
  59.5 13.8 %all-to-all-start.1 = ((f32[9,16,256]{2,0,1:T(8,128)}), f32[9,16,256]{2,0,1:T(8,128)S(1)}, u32[]{:S(2)}, u32[]{:S(2)}) async-start(f32[9,16,256]{2,0,1:T(8,128)} %multiply_bitcast_fusion), calls=%async_computation.1 | async-start | bytes 524288 | tf_op jit(solution)/shard_map/all_to_all | solution.py:118
  63.7 5.5 %collective-permute-start.2 = (f32[9,4,256]{2,0,1:T(8,128)S(1)}, f32[9,4,256]{2,0,1:T(8,128)S(1)}, u32[]{:S(2)}, u32[]{:S(2)}) collective-permute-start(f32[9,4,256]{2,0,1:T(8,128)S(1)} %get-tuple-element.202), channel_id=1, source_target_pairs={{0,8},{8,16},{16,24},{1,9},{9,17},{17,25},{2,10},{10,18},{18,26},{... | collective-permute-start | bytes 110600 | tf_op jit(solution)/shard_map/ppermute | solution.py:25
  67.2 6.2 %collective-permute-start.3 = (f32[9,4,256]{2,0,1:T(8,128)S(1)}, f32[9,4,256]{2,0,1:T(8,128)S(1)}, u32[]{:S(2)}, u32[]{:S(2)}) collective-permute-start(f32[9,4,256]{2,0,1:T(8,128)S(1)} %get-tuple-element.203), channel_id=1, source_target_pairs={{8,0},{16,8},{24,16},{9,1},{17,9},{25,17},{10,2},{18,10},{26,18},{... | collective-permute-start | bytes 110600 | tf_op jit(solution)/shard_map/ppermute | solution.py:27
  73.4 81.8 %copy-start = (f32[3,32,256]{2,1,0:T(8,128)S(1)}, f32[3,32,256]{2,1,0:T(8,128)}, u32[]{:S(2)}) copy-start(f32[3,32,256]{2,1,0:T(8,128)} %param.13) | copy-start | bytes 294916
  73.5 81.8 %copy-start.5 = (f32[3]{0:T(128)S(1)}, f32[3]{0:T(128)}, u32[]{:S(2)}) copy-start(f32[3]{0:T(128)} %constant.123) | copy-start | bytes 40
  157.1 4.0 %collective-permute-start.4 = (f32[7,2,256]{2,0,1:T(8,128)S(1)}, f32[7,2,256]{2,0,1:T(8,128)S(1)}, u32[]{:S(2)}, u32[]{:S(2)}) collective-permute-start(f32[7,2,256]{2,0,1:T(8,128)S(1)} %get-tuple-element.212), channel_id=1, source_target_pairs={{0,1},{1,0},{2,3},{3,2},{4,5},{5,4},{6,7},{7,6},{8,9},{9,8},{10,11... | collective-permute-start | bytes 43016 | tf_op jit(solution)/shard_map/ppermute | solution.py:163
  157.2 6.5 %collective-permute-start.5 = (f32[7,2,256]{2,0,1:T(8,128)S(1)}, f32[7,2,256]{2,0,1:T(8,128)S(1)}, u32[]{:S(2)}, u32[]{:S(2)}) collective-permute-start(f32[7,2,256]{2,0,1:T(8,128)S(1)} %get-tuple-element.211), channel_id=1, source_target_pairs={{0,2},{1,3},{2,0},{3,1},{4,6},{5,7},{6,4},{7,5},{8,10},{9,11},{10,... | collective-permute-start | bytes 43016 | tf_op jit(solution)/shard_map/ppermute | solution.py:163
  159.3 4.5 %collective-permute-start.6 = (f32[7,2,256]{2,0,1:T(8,128)S(1)}, f32[7,2,256]{2,0,1:T(8,128)S(1)}, u32[]{:S(2)}, u32[]{:S(2)}) collective-permute-start(f32[7,2,256]{2,0,1:T(8,128)S(1)} %get-tuple-element.210), channel_id=1, source_target_pairs={{0,3},{1,2},{2,1},{3,0},{4,7},{5,6},{6,5},{7,4},{8,11},{9,10},{10,... | collective-permute-start | bytes 43016 | tf_op jit(solution)/shard_map/ppermute | solution.py:163
  159.4 4.5 %collective-permute-start.7 = (f32[7,2,256]{2,0,1:T(8,128)S(1)}, f32[7,2,256]{2,0,1:T(8,128)S(1)}, u32[]{:S(2)}, u32[]{:S(2)}) collective-permute-start(f32[7,2,256]{2,0,1:T(8,128)S(1)} %get-tuple-element.209), channel_id=1, source_target_pairs={{0,4},{1,5},{2,6},{3,7},{4,0},{5,1},{6,2},{7,3},{8,12},{9,13},{10,... | collective-permute-start | bytes 43016 | tf_op jit(solution)/shard_map/ppermute | solution.py:163
  161.1 3.2 %collective-permute-start.8 = (f32[7,2,256]{2,0,1:T(8,128)S(1)}, f32[7,2,256]{2,0,1:T(8,128)S(1)}, u32[]{:S(2)}, u32[]{:S(2)}) collective-permute-start(f32[7,2,256]{2,0,1:T(8,128)S(1)} %get-tuple-element.208), channel_id=1, source_target_pairs={{0,5},{1,4},{2,7},{3,6},{4,1},{5,0},{6,3},{7,2},{8,13},{9,12},{10,... | collective-permute-start | bytes 43016 | tf_op jit(solution)/shard_map/ppermute | solution.py:163
  161.1 4.6 %collective-permute-start.9 = (f32[7,2,256]{2,0,1:T(8,128)S(1)}, f32[7,2,256]{2,0,1:T(8,128)S(1)}, u32[]{:S(2)}, u32[]{:S(2)}) collective-permute-start(f32[7,2,256]{2,0,1:T(8,128)S(1)} %get-tuple-element.207), channel_id=1, source_target_pairs={{0,6},{1,7},{2,4},{3,5},{4,2},{5,3},{6,0},{7,1},{8,14},{9,15},{10,... | collective-permute-start | bytes 43016 | tf_op jit(solution)/shard_map/ppermute | solution.py:163
  163.7 4.1 %collective-permute-start.10 = (f32[7,2,256]{2,0,1:T(8,128)S(1)}, f32[7,2,256]{2,0,1:T(8,128)S(1)}, u32[]{:S(2)}, u32[]{:S(2)}) collective-permute-start(f32[7,2,256]{2,0,1:T(8,128)S(1)} %get-tuple-element.206), channel_id=1, source_target_pairs={{0,7},{1,6},{2,5},{3,4},{4,3},{5,2},{6,1},{7,0},{8,15},{9,14},{10,... | collective-permute-start | bytes 43016 | tf_op jit(solution)/shard_map/ppermute | solution.py:163
